TPU v7x, 32 devices: a whole 2x2x4 slice. The times are simulated.
32 devices in a mesh: groups: 2 (over y), seq: 4 (over z), mp: 2 (over x), branch: 2 (over core).
Axes of the slice: x: 2, y: 2, z: 4, core: 2. Of those that a mesh axis runs over, the one named last changes fastest.
Arguments:
- streams: float32 [2, 8, 256, 1152], P('branch', ('groups', 'seq')), parts along dimension 1, may hold values from -6 to 6
- modulation: float32 [2, 6, 1152], P('branch'), may hold values from -3 to 3
- s_qkv: bfloat16 [2, 1152, 3, 1152], P('branch', 'seq', None, 'mp'), may hold values from -0.1875 to 0.1875
- s_out: bfloat16 [2, 1152, 1152], P('branch', 'mp', 'seq'), may hold values from -0.25 to 0.25
- w_in: bfloat16 [2, 1152, 4608], P('branch', 'seq', 'mp'), may hold values from -0.1875 to 0.1875
- w_out: bfloat16 [2, 4608, 1152], P('branch', 'mp', 'seq'), may hold values from -0.125 to 0.125
- hint_gain: float32 [13, 1152], replicated, may hold values from 0.3 to 3
- inject_layer: int32 [4], replicated, may hold values from 0 to 12
- hint_weight: bfloat16 [1152, 1152], P('seq', 'mp'), may hold values from -0.1875 to 0.1875
- t_mod: float32 [3, 1152], replicated, may hold values from -3 to 3
- t_qkv: bfloat16 [1152, 3, 1152], P('seq', None, 'mp'), may hold values from -0.1875 to 0.1875
- t_out: bfloat16 [1152, 1152], P('mp', 'seq'), may hold values from -0.25 to 0.25
Outputs:
- main_out: float32 [8, 256, 1152], P('groups', ('seq', 'branch'), 'mp'), parts along dimension 0
There are 2 independent parts, one for each index of `groups`. A program takes and returns all parts, laid end to end along the dimension named above; an argument that names none is the same for every part. Nothing has to cross between parts.
All inputs are finite; a program needn't handle non-finite values.
Results may differ from a plain program's by a relative error of at most 0.014.
Values may be sent and summed in bfloat16 or wider, within the bound.
No kernel may reach another device: no remote copies, remote signals or barrier semaphores. Data moves between devices by JAX's collectives and lax.ppermute only.
A program may use at most 64 MiB of HBM per device.

v0:
```python
import jax
import jax.numpy as jnp
from jax import lax
from jax.sharding import PartitionSpec as P

D = 1152
HEAD_DIM = 72
HINT_LAYERS = 13


def layer_norm(value, shift, scale):
    mean = jnp.mean(value, axis=-1, keepdims=True)
    centred = value - mean
    var = jnp.mean(centred * centred, axis=-1, keepdims=True)
    return centred * lax.rsqrt(var + 1e-06) * (1.0 + scale) + shift


def attend(query, keys, values):
    scores = jnp.einsum("qhd,khd->hqk", query, keys, precision=lax.Precision.HIGHEST) / jnp.sqrt(
        jnp.float32(HEAD_DIM)
    )
    weights = jnp.exp(scores)
    weights = weights / jnp.sum(weights, axis=-1, keepdims=True)
    result = jnp.einsum("hqk,khd->qhd", weights, values, precision=lax.Precision.HIGHEST)
    return result.reshape(result.shape[0], -1)


def row_product(left, piece):
    return jnp.dot(left, piece, preferred_element_type=jnp.float32)


def on_device(
    streams,
    modulation,
    s_qkv,
    s_out,
    w_in,
    w_out,
    hint_gain,
    inject_layer,
    hint_weight,
    t_mod,
    t_qkv,
    t_out,
):
    stream = streams[0, 0]
    mods = modulation[0]
    tokens = stream.shape[0]
    quarter = s_qkv.shape[3]
    offset = lax.axis_index("mp") * quarter
    local_heads = quarter // HEAD_DIM

    def share(vector):
        return lax.dynamic_slice_in_dim(vector, offset, quarter, 0)

    normed = layer_norm(stream, mods[0], mods[1]).astype(jnp.bfloat16)
    piece = lax.all_gather(s_qkv, "seq", axis=1, tiled=True)
    qkv = row_product(normed, piece[0].reshape(piece.shape[1], 3 * quarter))
    qkv = qkv.reshape(tokens, 3, local_heads, HEAD_DIM)
    attended = attend(qkv[:, 0], qkv[:, 1], qkv[:, 2]).astype(jnp.bfloat16)
    projected = jnp.dot(
        attended,
        lax.all_gather(s_out, "seq", axis=2, tiled=True)[0],
        preferred_element_type=jnp.float32,
    )
    partial_value = lax.psum_scatter(
        projected.astype(jnp.bfloat16), "mp", scatter_dimension=1, tiled=True
    ).astype(jnp.float32)
    stream_share = (
        lax.dynamic_slice_in_dim(stream, offset, quarter, 1) + share(mods[2]) * partial_value
    )
    stream = lax.all_gather(stream_share.astype(jnp.bfloat16), "mp", axis=1, tiled=True).astype(
        stream_share.dtype
    )
    normed = layer_norm(stream, mods[3], mods[4]).astype(jnp.bfloat16)
    upward = row_product(normed, lax.all_gather(w_in, "seq", axis=1, tiled=True)[0])
    hidden = jax.nn.gelu(upward, approximate=True).astype(jnp.bfloat16)
    downward = jnp.dot(
        hidden,
        lax.all_gather(w_out, "seq", axis=2, tiled=True)[0],
        preferred_element_type=jnp.float32,
    )
    mlp_part = lax.psum_scatter(
        downward.astype(jnp.bfloat16), "mp", scatter_dimension=1, tiled=True
    ).astype(jnp.float32)
    section_out = stream_share + share(mods[5]) * mlp_part
    moved = lax.all_to_all(
        lax.all_to_all(
            section_out[None, None].astype(jnp.bfloat16),
            "seq",
            split_axis=2,
            concat_axis=1,
            tiled=True,
        ),
        "branch",
        split_axis=2,
        concat_axis=0,
        tiled=True,
    ).astype(jnp.float32)
    frames = moved.shape[1]
    positions = moved.shape[2]
    rows = frames * positions
    control = moved[0]
    main_share = moved[1].reshape(rows, quarter)
    picks = (inject_layer[:, None] == jnp.arange(HINT_LAYERS, dtype=jnp.int32)[None, :]).astype(
        jnp.float32
    )
    gain = jnp.sum(picks[:, :, None] * hint_gain[None, :, :], axis=1)
    control_whole = lax.all_gather(control.astype(jnp.bfloat16), "mp", axis=2, tiled=True).astype(
        control.dtype
    )
    hint_in = (control_whole * gain[:, None, :]).astype(jnp.bfloat16).reshape(rows, D)
    hint = row_product(hint_in, lax.all_gather(hint_weight, "seq", axis=0, tiled=True))
    joined_share = main_share + hint
    joined = lax.all_gather(joined_share.astype(jnp.bfloat16), "mp", axis=1, tiled=True).astype(
        joined_share.dtype
    )
    normed_t = layer_norm(joined, t_mod[0], t_mod[1]).astype(jnp.bfloat16)
    piece = lax.all_gather(t_qkv, "seq", axis=0, tiled=True)
    tqkv = row_product(normed_t, piece.reshape(piece.shape[0], 3 * quarter))
    tqkv = tqkv.reshape(frames, positions, 3, local_heads, HEAD_DIM).transpose(1, 0, 2, 3, 4)
    attended_t = jax.vmap(attend)(tqkv[:, :, 0], tqkv[:, :, 1], tqkv[:, :, 2])
    attended_t = attended_t.transpose(1, 0, 2).reshape(rows, quarter).astype(jnp.bfloat16)
    projected_t = jnp.dot(
        attended_t,
        lax.all_gather(t_out, "seq", axis=1, tiled=True),
        preferred_element_type=jnp.float32,
    )
    temporal_part = lax.psum_scatter(
        projected_t.astype(jnp.bfloat16), "mp", scatter_dimension=1, tiled=True
    ).astype(jnp.float32)
    result = joined_share + share(t_mod[2]) * temporal_part
    return result.reshape(frames, positions, quarter)


def solution(mesh):
    in_specs = (
        P("branch", ("groups", "seq"), None, None),
        P("branch", None, None),
        P("branch", "seq", None, "mp"),
        P("branch", "mp", "seq"),
        P("branch", "seq", "mp"),
        P("branch", "mp", "seq"),
        P(),
        P(),
        P("seq", "mp"),
        P(),
        P("seq", None, "mp"),
        P("mp", "seq"),
    )
    out_specs = P("groups", ("seq", "branch"), "mp")
    return jax.shard_map(
        on_device, mesh=mesh, in_specs=in_specs, out_specs=out_specs, check_vma=False
    )
```

profile of v0, /device:TPU:0, one launch (start us, length us, event | category | flops | bytes accessed | tf_op | source)
XLA Modules:
  0.0 556.1 jit_solution(1745419225290000428)
XLA Ops:
  8.6 87.6 %all-gather.9.cloned.1.call-done = bf16[1,1152,3,576]{3,1,2,0:T(8,128)(2,1)} async-done(((bf16[1,288,3,576]{3,1,2,0:T(8,128)(2,1)}), bf16[1,1152,3,576]{3,1,2,0:T(8,128)(2,1)}) %all-gather.9.cloned.1.call-update) | async-done | bytes 3981328 | tf_op jit(solution)/shard_map/all_gather | solution.py:57
  96.2 6.6 %copy.53 = bf16[1,1152,3,576]{1,3,2,0:T(8,128)(2,1)} copy(bf16[1,1152,3,576]{3,1,2,0:T(8,128)(2,1)} %all-gather.9.cloned.1.call-done) | data formatting | bytes 7962624 | tf_op jit(solution)/shard_map/all_gather | solution.py:57
  102.8 3.8 fusion.45
  106.6 2.1 fusion.21
  108.7 1.7 fusion.26
  110.4 21.2 %all-gather.11.cloned.1.call-done = bf16[1,576,1152]{1,2,0:T(8,128)(2,1)} async-done(((bf16[1,576,288]{1,2,0:T(8,128)(2,1)}), bf16[1,576,1152]{1,2,0:T(8,128)(2,1)}) %all-gather.11.cloned.1.call-update) | async-done | bytes 1327120 | tf_op jit(solution)/shard_map/all_gather | solution.py:63
  131.6 2.8 convolution_convert_fusion
  136.2 12.7 %reduce-scatter.4.cloned.1.call-done = bf16[256,576]{0,1:T(8,128)(2,1)} async-done(((bf16[256,1152]{0,1:T(8,128)(2,1)}), bf16[256,576]{0,1:T(8,128)(2,1)}) %reduce-scatter.4.cloned.1.call-update) | async-done | bytes 294928 | tf_op jit(solution)/shard_map/reduce_scatter | solution.py:66
  148.9 1.1 fusion.70
  150.0 9.3 %all_gather.32 = bf16[256,1152]{0,1:T(8,128)(2,1)S(1)} all-gather(bf16[256,576]{0,1:T(8,128)(2,1)S(1)} %fusion.70), channel_id=1, replica_groups=mesh['groups'=2,'seq'=4,'mp'=2,'branch'=2] {'mp'}, dimensions={1}, use_global_device_ids=true | all-gather | bytes 884736 | tf_op jit(solution)/shard_map/all_gather | solution.py:72
  159.6 89.8 %all-gather.13.cloned.1.call-done = bf16[1,1152,2304]{2,1,0:T(8,128)(2,1)} async-done(((bf16[1,288,2304]{2,1,0:T(8,128)(2,1)}), bf16[1,1152,2304]{2,1,0:T(8,128)(2,1)}) %all-gather.13.cloned.1.call-update) | async-done | bytes 5308432 | tf_op jit(solution)/shard_map/all_gather | solution.py:76
  249.5 98.9 %all-gather.15.cloned.1.call-done = bf16[1,2304,1152]{1,2,0:T(8,128)(2,1)} async-done(((bf16[1,2304,288]{1,2,0:T(8,128)(2,1)}), bf16[1,2304,1152]{1,2,0:T(8,128)(2,1)}) %all-gather.15.cloned.1.call-update) | async-done | bytes 5308432 | tf_op jit(solution)/shard_map/all_gather | solution.py:80
  348.4 8.2 %fusion.4 = bf16[256,1152]{0,1:T(8,128)(2,1)} fusion(bf16[1,2304,1152]{1,2,0:T(8,128)(2,1)} %all-gather.15.cloned.1.call-done, bf16[1,1152,2304]{2,1,0:T(8,128)(2,1)} %all-gather.13.cloned.1.call-done, bf16[256,1152]{0,1:T(8,128)(2,1)S(1)} %all_gather.32, f32[1152]{0:T(1024)S(1)} %get-tuple-element.18, f32[1152]{0:T(1024)S(1)} %get-tuple-element.21, ...), kind=kOutput, calls=%fused_computation.6 | convolution fusion | flops 2725281792 | bytes 11807744 | tf_op jit(solution)/shard_map/dot_general | solution.py:78
  358.9 11.5 %reduce-scatter.6.cloned.1.call-done = bf16[256,576]{0,1:T(8,128)(2,1)} async-done(((bf16[256,1152]{0,1:T(8,128)(2,1)}), bf16[256,576]{0,1:T(8,128)(2,1)}) %reduce-scatter.6.cloned.1.call-update) | async-done | bytes 294928 | tf_op jit(solution)/shard_map/reduce_scatter | solution.py:83
  370.4 1.2 fusion.71
  372.8 2.7 reduce.19
  375.5 1.1 reshape.175
  376.6 4.6 all-to-all-start
  381.4 81.1 %all-gather.19.cloned.1.call-done = bf16[1152,3,576]{2,0,1:T(8,128)(2,1)} async-done(((bf16[288,3,576]{2,0,1:T(8,128)(2,1)}), bf16[1152,3,576]{2,0,1:T(8,128)(2,1)}) %all-gather.19.cloned.1.call-update) | async-done | bytes 3981328 | tf_op jit(solution)/shard_map/all_gather | solution.py:119
  462.4 6.6 %copy.62 = bf16[1152,3,576]{0,2,1:T(8,128)(2,1)} copy(bf16[1152,3,576]{2,0,1:T(8,128)(2,1)} %all-gather.19.cloned.1.call-done) | data formatting | bytes 7962624 | tf_op jit(solution)/shard_map/all_gather | solution.py:119
  469.9 4.0 all_to_all.21
  474.3 16.0 %all-gather = bf16[1,1,4,32,1152]{3,2,1,0,4:T(4,128)(2,1)S(1)} all-gather(bf16[1,1,4,32,576]{3,2,1,0,4:T(4,128)(2,1)S(1)} %copy.58), channel_id=2, replica_groups=mesh['groups'=2,'seq'=4,'mp'=2,'branch'=2] {'mp'}, dimensions={4}, use_global_device_ids=true | all-gather | bytes 442368 | tf_op jit(solution)/shard_map/all_gather | solution.py:109
  490.4 1.2 copy.59
  491.8 5.7 %all-gather.17.cloned.1.call-done = bf16[1152,576]{1,0:T(8,128)(2,1)} async-done(((bf16[288,576]{1,0:T(8,128)(2,1)}), bf16[1152,576]{1,0:T(8,128)(2,1)}) %all-gather.17.cloned.1.call-update) | async-done | bytes 1327120 | tf_op jit(solution)/shard_map/all_gather | solution.py:113
  497.5 2.0 fusion.83
  499.6 6.0 %all_gather.37 = bf16[128,1152]{0,1:T(8,128)(2,1)S(1)} all-gather(bf16[128,576]{0,1:T(8,128)(2,1)S(1)} %get-tuple-element.25), channel_id=1, replica_groups=mesh['groups'=2,'seq'=4,'mp'=2,'branch'=2] {'mp'}, dimensions={1}, use_global_device_ids=true | all-gather | bytes 442368 | tf_op jit(solution)/shard_map/all_gather | solution.py:115
  506.5 4.3 convolution_bitcast_fusion
  511.0 2.5 fusion.25
  513.5 2.6 fusion.35
  516.4 17.1 %all-gather.21.cloned.1.call-done = bf16[576,1152]{0,1:T(8,128)(2,1)} async-done(((bf16[576,288]{0,1:T(8,128)(2,1)}), bf16[576,1152]{0,1:T(8,128)(2,1)}) %all-gather.21.cloned.1.call-update) | async-done | bytes 1327120 | tf_op jit(solution)/shard_map/all_gather | solution.py:126
  533.4 2.6 convolution_convert_fusion.1
  536.2 11.1 %reduce-scatter.8.cloned.1.call-done = bf16[128,576]{0,1:T(8,128)(2,1)} async-done(((bf16[128,1152]{0,1:T(8,128)(2,1)}), bf16[128,576]{0,1:T(8,128)(2,1)}) %reduce-scatter.8.cloned.1.call-update) | async-done | bytes 147472 | tf_op jit(solution)/shard_map/reduce_scatter | solution.py:129
  (72 shorter events, 12.5 us)
Async XLA Ops:
  6.5 1.5 copy-start
  6.5 89.6 %all-gather.9.cloned.1.call-start = ((), (), s32[]{:S(2)}) async-start(), calls=%async_computation.5 | async-start | bytes 5529600 | tf_op jit(solution)/shard_map/all_gather | solution.py:57
  7.3 1.2 copy-start.3
  7.3 124.3 %all-gather.11.cloned.1.call-start = ((), (), s32[]{:S(2)}) async-start(), calls=%async_computation.6 | async-start | bytes 1843200 | tf_op jit(solution)/shard_map/all_gather | solution.py:63
  8.0 140.9 %reduce-scatter.4.cloned.1.call-start = ((), (), s32[]{:S(2)}) async-start(), calls=%async_computation.7 | async-start | bytes 884736 | tf_op jit(solution)/shard_map/reduce_scatter | solution.py:66
  134.4 115.1 %all-gather.13.cloned.1.call-start = ((), (), s32[]{:S(2)}) async-start(), calls=%async_computation.8 | async-start | bytes 6635520 | tf_op jit(solution)/shard_map/all_gather | solution.py:76
  135.0 213.4 %all-gather.15.cloned.1.call-start = ((), (), s32[]{:S(2)}) async-start(), calls=%async_computation.9 | async-start | bytes 6635520 | tf_op jit(solution)/shard_map/all_gather | solution.py:80
  135.6 234.8 %reduce-scatter.6.cloned.1.call-start = ((), (), s32[]{:S(2)}) async-start(), calls=%async_computation.10 | async-start | bytes 884736 | tf_op jit(solution)/shard_map/reduce_scatter | solution.py:83
  356.6 13.9 %copy-start.1 = (bf16[256,576]{0,1:T(8,128)(2,1)S(1)}, bf16[256,576]{0,1:T(8,128)(2,1)}, u32[]{:S(2)}) copy-start(bf16[256,576]{0,1:T(8,128)(2,1)} %reduce-scatter.4.cloned.1.call-done) | copy-start | bytes 884740
  356.6 105.8 %all-gather.19.cloned.1.call-start = ((), (), s32[]{:S(2)}) async-start(), calls=%async_computation.12 | async-start | bytes 5529600 | tf_op jit(solution)/shard_map/all_gather | solution.py:119
  357.4 140.2 %all-gather.17.cloned.1.call-start = ((), (), s32[]{:S(2)}) async-start(), calls=%async_computation.11 | async-start | bytes 1843200 | tf_op jit(solution)/shard_map/all_gather | solution.py:113
  358.1 175.3 %all-gather.21.cloned.1.call-start = ((), (), s32[]{:S(2)}) async-start(), calls=%async_computation.13 | async-start | bytes 1843200 | tf_op jit(solution)/shard_map/all_gather | solution.py:126
  371.6 9.6 %copy-start.5 = (s32[4]{0:T(128)S(1)}, s32[4]{0:T(128)}, u32[]{:S(2)}) copy-start(s32[4]{0:T(128)} %param.19) | copy-start | bytes 52
  371.6 9.5 %copy-start.2 = (f32[13,1152]{1,0:T(8,128)S(1)}, f32[13,1152]{1,0:T(8,128)}, u32[]{:S(2)}) copy-start(f32[13,1152]{1,0:T(8,128)} %param.18) | copy-start | bytes 179716
  371.7 9.7 %copy-start.4 = (f32[3,1152]{1,0:T(4,128)S(1)}, f32[3,1152]{1,0:T(4,128)}, u32[]{:S(2)}) copy-start(f32[3,1152]{1,0:T(4,128)} %param.21) | copy-start | bytes 41476
  376.6 92.4 %all-to-all-start = ((bf16[4,2,18432]{2,1,0:T(2,128)(2,1)}), bf16[4,2,18432]{2,1,0:T(2,128)(2,1)S(1)}, u32[]{:S(2)}, u32[]{:S(2)}) async-start(bf16[4,2,18432]{2,1,0:T(2,128)(2,1)} %reshape.175), calls=%async_computation.2 | async-start | bytes 589824 | tf_op jit(solution)/shard_map/all_to_all | solution.py:88
  381.2 166.1 %reduce-scatter.8.cloned.1.call-start = ((), (), s32[]{:S(2)}) async-start(), calls=%async_computation.14 | async-start | bytes 442368 | tf_op jit(solution)/shard_map/reduce_scatter | solution.py:129
Sparse Core Ops, SparseCore 0:
  8.9 87.2 all-gather.8
  97.7 33.7 all-gather.10
  134.5 14.2 reduce-scatter.3
  150.3 99.1 all-gather.12
  250.9 97.4 all-gather.14
  356.7 13.6 reduce-scatter.5
  372.0 90.3 all-gather.18
  464.0 33.4 all-gather.16
  499.1 34.2 all-gather.20
  536.2 11.0 reduce-scatter.7
where the time goes:
time: 557 us; the launch traced here: 556 us
  waiting for transfers between devices  441 us (79%)
  blocking collectives  35.3 us (6%)
  matrix products  32.7 us (6%)
  local copies, waits for them, and re-layouts  20.2 us (4%)
  between operations  13.8 us (2%)
  other arithmetic  7.89 us (1%)
    all_gather x1, waiting for transfers between devices, on_device(): lax.all_gather(w_out, 'seq', axis=2, tiled=True)[0]  98.9 us
    all_gather x1, waiting for transfers between devices, on_device(): lax.all_gather(w_in, 'seq', axis=1, tiled=True)[0]  89.8 us
    all_gather x1, waiting for transfers between devices, on_device(): piece = lax.all_gather(s_qkv, 'seq', axis=1, tiled=True)  87.6 us
    all_gather x1, waiting for transfers between devices, on_device(): piece = lax.all_gather(t_qkv, 'seq', axis=0, tiled=True)  81.1 us
    all_gather x1, waiting for transfers between devices, on_device(): lax.all_gather(s_out, 'seq', axis=2, tiled=True)[0]  21.2 us
    all_gather x1, waiting for transfers between devices, on_device(): lax.all_gather(t_out, 'seq', axis=1, tiled=True)  17.1 us
    all_gather x1, blocking collectives, on_device(): lax.all_gather(control.astype(jnp.bfloat16), 'mp', axis=2, tiled=True)  16 us
    reduce_scatter x1, waiting for transfers between devices, on_device(): lax.psum_scatter(projected.astype(jnp.bfloat16), 'mp', scatter_dimension=...  12.7 us
  transfers between devices with their start and end apart: 11, of which 10 were waited for; matrix products, arithmetic and copies ran while one was open for 8% of the time, Pallas kernels for 0%

commit v1 on v0

--- a/solution.py
+++ b/solution.py
@@ -6,6 +6,17 @@
 D = 1152
 HEAD_DIM = 72
 HINT_LAYERS = 13
+
+
+def collect(x, axis, dim):
+    ways = lax.axis_size(axis)
+    pieces = [x]
+    for far in range(1, ways):
+        pieces.append(
+            lax.ppermute(pieces[far - 1], axis, [(d, (d - 1) % ways) for d in range(ways)])
+        )
+    line = jnp.concatenate(pieces, axis=dim)
+    return jnp.roll(line, lax.axis_index(axis) * x.shape[dim], axis=dim)
 
 
 def layer_norm(value, shift, scale):
@@ -73,7 +84,7 @@
         stream_share.dtype
     )
     normed = layer_norm(stream, mods[3], mods[4]).astype(jnp.bfloat16)
-    upward = row_product(normed, lax.all_gather(w_in, "seq", axis=1, tiled=True)[0])
+    upward = row_product(normed, collect(w_in, "seq", 1)[0])
     hidden = jax.nn.gelu(upward, approximate=True).astype(jnp.bfloat16)
     downward = jnp.dot(
         hidden,

time: 557 us -> 539 us (0.968)
  waiting for transfers between devices: 441 us -> 405 us
  local copies, waits for them, and re-layouts: 20.2 us -> 37.8 us
    ppermute x0 -> x3, waiting for transfers between devices: none -> 163 us  [collect(): lax.ppermute(pieces[far - 1], axis, [(d, (d - 1) % ways) for d in range(w...]
    all_gather x1, waiting for transfers between devices: 98.9 us -> 0.01 us  [on_device(): lax.all_gather(w_out, 'seq', axis=2, tiled=True)[0]]
    all_gather x1 -> x0, waiting for transfers between devices: 89.8 us -> none  [on_device(): lax.all_gather(w_in, 'seq', axis=1, tiled=True)[0]]
    unnamed x16 -> x29, local copies, waits for them, and re-layouts: 2.24 us -> 17.4 us
    reduce_scatter x1, waiting for transfers between devices: 12.7 us -> 0.01 us  [on_device(): lax.psum_scatter(projected.astype(jnp.bfloat16), 'mp', scatter_dimension=...]
  transfers between devices with their start and end apart: 11 -> 13, of which waited for: 10 -> 10; matrix products, arithmetic and copies ran while one was open for 8% -> 11% of each run, Pallas kernels for 0% -> 0%
where the time goes in v1:
time: 539 us; the launch traced here: 538 us
  waiting for transfers between devices  405 us (75%)
  local copies, waits for them, and re-layouts  37.8 us (7%)
  blocking collectives  34 us (6%)
  matrix products  33 us (6%)
  between operations  13.5 us (3%)
  other arithmetic  7.89 us (1%)
  starting transfers between devices  6.89 us (1%)
    ppermute x3, waiting for transfers between devices, collect(): lax.ppermute(pieces[far - 1], axis, [(d, (d - 1) % ways) for d in range(w...  163 us
    all_gather x1, waiting for transfers between devices, on_device(): piece = lax.all_gather(s_qkv, 'seq', axis=1, tiled=True)  87.6 us
    all_gather x1, waiting for transfers between devices, on_device(): piece = lax.all_gather(t_qkv, 'seq', axis=0, tiled=True)  81.1 us
    all_gather x1, waiting for transfers between devices, on_device(): lax.all_gather(s_out, 'seq', axis=2, tiled=True)[0]  21.2 us
    unnamed x29, local copies, waits for them, and re-layouts  17.4 us
    all_gather x1, waiting for transfers between devices, on_device(): lax.all_gather(t_out, 'seq', axis=1, tiled=True)  17.1 us
    all_gather x1, blocking collectives, on_device(): lax.all_gather(control.astype(jnp.bfloat16), 'mp', axis=2, tiled=True)  16 us
    reduce_scatter x1, waiting for transfers between devices, on_device(): lax.psum_scatter(downward.astype(jnp.bfloat16), 'mp', scatter_dimension=1...  14.8 us
  transfers between devices with their start and end apart: 13, of which 10 were waited for; matrix products, arithmetic and copies ran while one was open for 11% of the time, Pallas kernels for 0%

profile of v1, /device:TPU:0, one launch (start us, length us, event | category | flops | bytes accessed | tf_op | source)
XLA Modules:
  0.0 538.3 jit_solution(9252212746418876748)
XLA Ops:
  8.6 87.6 %all-gather.8.cloned.1.call-done = bf16[1,1152,3,576]{3,1,2,0:T(8,128)(2,1)} async-done(((bf16[1,288,3,576]{3,1,2,0:T(8,128)(2,1)}), bf16[1,1152,3,576]{3,1,2,0:T(8,128)(2,1)}) %all-gather.8.cloned.1.call-update) | async-done | bytes 3981328 | tf_op jit(solution)/shard_map/all_gather | solution.py:68
  96.2 6.6 %copy.53 = bf16[1,1152,3,576]{1,3,2,0:T(8,128)(2,1)} copy(bf16[1,1152,3,576]{3,1,2,0:T(8,128)(2,1)} %all-gather.8.cloned.1.call-done) | data formatting | bytes 7962624 | tf_op jit(solution)/shard_map/all_gather | solution.py:68
  102.8 3.8 fusion.52
  106.6 2.1 fusion.22
  110.4 21.2 %all-gather.10.cloned.1.call-done = bf16[1,576,1152]{1,2,0:T(8,128)(2,1)} async-done(((bf16[1,576,288]{1,2,0:T(8,128)(2,1)}), bf16[1,576,1152]{1,2,0:T(8,128)(2,1)}) %all-gather.10.cloned.1.call-update) | async-done | bytes 1327120 | tf_op jit(solution)/shard_map/all_gather | solution.py:74
  131.6 2.9 convolution_convert_fusion
  136.6 38.6 %collective-permute-done = bf16[1,288,2304]{2,1,0:T(8,128)(2,1)S(1)} collective-permute-done((bf16[1,288,2304]{2,1,0:T(8,128)(2,1)S(1)}, bf16[1,288,2304]{2,1,0:T(8,128)(2,1)S(1)}, u32[]{:S(2)}, u32[]{:S(2)}) %collective-permute-start) | collective-permute-done | bytes 1327136 | tf_op jit(solution)/shard_map/ppermute | solution.py:16
  176.8 90.8 %collective-permute-done.1 = bf16[1,288,2304]{2,1,0:T(8,128)(2,1)} collective-permute-done((bf16[1,288,2304]{2,1,0:T(8,128)(2,1)S(1)}, bf16[1,288,2304]{2,1,0:T(8,128)(2,1)}, u32[]{:S(2)}, u32[]{:S(2)}) %collective-permute-start.1) | collective-permute-done | bytes 1327136 | tf_op jit(solution)/shard_map/ppermute | solution.py:16
  269.3 2.5 constant_dynamic-update-slice_fusion.6
  271.8 2.5 constant_dynamic-update-slice_fusion.5
  274.3 33.3 %collective-permute-done.2 = bf16[1,288,2304]{2,1,0:T(8,128)(2,1)} collective-permute-done((bf16[1,288,2304]{2,1,0:T(8,128)(2,1)}, bf16[1,288,2304]{2,1,0:T(8,128)(2,1)}, u32[]{:S(2)}, u32[]{:S(2)}) %collective-permute-start.2) | collective-permute-done | bytes 1327136 | tf_op jit(solution)/shard_map/ppermute | solution.py:16
  307.6 2.5 constant_dynamic-update-slice_fusion.4
  313.0 2.6 constant_dynamic-update-slice_fusion.1
  315.6 2.5 constant_dynamic-update-slice_fusion
  319.1 8.0 %all_gather.29 = bf16[256,1152]{0,1:T(8,128)(2,1)S(1)} all-gather(bf16[256,576]{0,1:T(8,128)(2,1)S(1)} %fusion.74), channel_id=1, replica_groups=mesh['groups'=2,'seq'=4,'mp'=2,'branch'=2] {'mp'}, dimensions={1}, use_global_device_ids=true | all-gather | bytes 884736 | tf_op jit(solution)/shard_map/all_gather | solution.py:83
  327.5 8.4 %fusion.5 = bf16[256,1152]{0,1:T(8,128)(2,1)} fusion(bf16[1,2304,1152]{1,2,0:T(8,128)(2,1)} %all-gather.12.cloned.1.call-done, bf16[1,2304,2304]{2,1,0:T(8,128)(2,1)} %constant_dynamic-update-slice_fusion, s32[]{:T(128)S(6)} %select_n.21, bf16[256,1152]{0,1:T(8,128)(2,1)S(1)} %all_gather.29, f32[1152]{0:T(1024)S(1)} %get-tuple-element.18, ...), kind=kOutput, calls=%fused_computation.7 | convolution fusion | flops 2725281792 | bytes 11807748 | tf_op jit(solution)/shard_map/dot_general | solution.py:89
  338.1 14.8 %reduce-scatter.6.cloned.1.call-done = bf16[256,576]{0,1:T(8,128)(2,1)} async-done(((bf16[256,1152]{0,1:T(8,128)(2,1)}), bf16[256,576]{0,1:T(8,128)(2,1)}) %reduce-scatter.6.cloned.1.call-update) | async-done | bytes 294928 | tf_op jit(solution)/shard_map/reduce_scatter | solution.py:94
  355.3 2.7 reduce.19
  359.1 4.6 all-to-all-start
  363.9 81.1 %all-gather.16.cloned.1.call-done = bf16[1152,3,576]{2,0,1:T(8,128)(2,1)} async-done(((bf16[288,3,576]{2,0,1:T(8,128)(2,1)}), bf16[1152,3,576]{2,0,1:T(8,128)(2,1)}) %all-gather.16.cloned.1.call-update) | async-done | bytes 3981328 | tf_op jit(solution)/shard_map/all_gather | solution.py:130
  445.0 6.6 %copy.62 = bf16[1152,3,576]{0,2,1:T(8,128)(2,1)} copy(bf16[1152,3,576]{2,0,1:T(8,128)(2,1)} %all-gather.16.cloned.1.call-done) | data formatting | bytes 7962624 | tf_op jit(solution)/shard_map/all_gather | solution.py:130
  452.4 4.0 all_to_all.21
  456.9 16.0 %all-gather = bf16[1,1,4,32,1152]{3,2,1,0,4:T(4,128)(2,1)S(1)} all-gather(bf16[1,1,4,32,576]{3,2,1,0,4:T(4,128)(2,1)S(1)} %copy.58), channel_id=2, replica_groups=mesh['groups'=2,'seq'=4,'mp'=2,'branch'=2] {'mp'}, dimensions={4}, use_global_device_ids=true | all-gather | bytes 442368 | tf_op jit(solution)/shard_map/all_gather | solution.py:120
  474.4 5.7 %all-gather.14.cloned.1.call-done = bf16[1152,576]{1,0:T(8,128)(2,1)} async-done(((bf16[288,576]{1,0:T(8,128)(2,1)}), bf16[1152,576]{1,0:T(8,128)(2,1)}) %all-gather.14.cloned.1.call-update) | async-done | bytes 1327120 | tf_op jit(solution)/shard_map/all_gather | solution.py:124
  480.1 2.0 fusion.89
  482.1 6.0 %all_gather.33 = bf16[128,1152]{0,1:T(8,128)(2,1)S(1)} all-gather(bf16[128,576]{0,1:T(8,128)(2,1)S(1)} %get-tuple-element.25), channel_id=1, replica_groups=mesh['groups'=2,'seq'=4,'mp'=2,'branch'=2] {'mp'}, dimensions={1}, use_global_device_ids=true | all-gather | bytes 442368 | tf_op jit(solution)/shard_map/all_gather | solution.py:126
  489.1 4.3 convolution_bitcast_fusion
  493.5 2.5 fusion.28
  496.1 2.6 fusion.42
  498.9 17.1 %all-gather.18.cloned.1.call-done = bf16[576,1152]{0,1:T(8,128)(2,1)} async-done(((bf16[576,288]{0,1:T(8,128)(2,1)}), bf16[576,1152]{0,1:T(8,128)(2,1)}) %all-gather.18.cloned.1.call-update) | async-done | bytes 1327120 | tf_op jit(solution)/shard_map/all_gather | solution.py:137
  516.0 2.6 convolution_convert_fusion.1
  518.7 11.1 %reduce-scatter.8.cloned.1.call-done = bf16[128,576]{0,1:T(8,128)(2,1)} async-done(((bf16[128,1152]{0,1:T(8,128)(2,1)}), bf16[128,576]{0,1:T(8,128)(2,1)}) %reduce-scatter.8.cloned.1.call-update) | async-done | bytes 147472 | tf_op jit(solution)/shard_map/reduce_scatter | solution.py:140
  (89 shorter events, 25.3 us)
Async XLA Ops:
  6.5 1.5 copy-start
  6.5 2.0 copy-start.6
  6.5 89.6 %all-gather.8.cloned.1.call-start = ((), (), s32[]{:S(2)}) async-start(), calls=%async_computation.5 | async-start | bytes 5529600 | tf_op jit(solution)/shard_map/all_gather | solution.py:68
  7.3 124.3 %all-gather.10.cloned.1.call-start = ((), (), s32[]{:S(2)}) async-start(), calls=%async_computation.6 | async-start | bytes 1843200 | tf_op jit(solution)/shard_map/all_gather | solution.py:74
  8.0 310.0 %reduce-scatter.4.cloned.1.call-start = ((), (), s32[]{:S(2)}) async-start(), calls=%async_computation.7 | async-start | bytes 884736 | tf_op jit(solution)/shard_map/reduce_scatter | solution.py:77
  131.6 3.6 copy-start.1
  134.5 193.0 %all-gather.12.cloned.1.call-start = ((), (), s32[]{:S(2)}) async-start(), calls=%async_computation.8 | async-start | bytes 6635520 | tf_op jit(solution)/shard_map/all_gather | solution.py:91
  135.1 217.9 %reduce-scatter.6.cloned.1.call-start = ((), (), s32[]{:S(2)}) async-start(), calls=%async_computation.9 | async-start | bytes 884736 | tf_op jit(solution)/shard_map/reduce_scatter | solution.py:94
  135.2 40.0 %collective-permute-start = (bf16[1,288,2304]{2,1,0:T(8,128)(2,1)S(1)}, bf16[1,288,2304]{2,1,0:T(8,128)(2,1)S(1)}, u32[]{:S(2)}, u32[]{:S(2)}) collective-permute-start(bf16[1,288,2304]{2,1,0:T(8,128)(2,1)S(1)} %copy-done.1), channel_id=1, source_target_pairs={{0,12},{4,0},{8,4},{12,8},{1,13},{5,1},{9,5},{13,9},{2,14},{6,2},{... | collective-permute-start | bytes 3981320 | tf_op jit(solution)/shard_map/ppermute | solution.py:16
  175.1 1.1 copy-start.2
  176.2 91.3 %collective-permute-start.1 = (bf16[1,288,2304]{2,1,0:T(8,128)(2,1)S(1)}, bf16[1,288,2304]{2,1,0:T(8,128)(2,1)}, u32[]{:S(2)}, u32[]{:S(2)}) collective-permute-start(bf16[1,288,2304]{2,1,0:T(8,128)(2,1)S(1)} %collective-permute-done), channel_id=1, source_target_pairs={{0,12},{4,0},{8,4},{12,8},{1,13},{5,1},{9,5},{13,9},{2,14},{6,2},{... | collective-permute-start | bytes 3981320 | tf_op jit(solution)/shard_map/ppermute | solution.py:16
  267.6 40.0 %collective-permute-start.2 = (bf16[1,288,2304]{2,1,0:T(8,128)(2,1)}, bf16[1,288,2304]{2,1,0:T(8,128)(2,1)}, u32[]{:S(2)}, u32[]{:S(2)}) collective-permute-start(bf16[1,288,2304]{2,1,0:T(8,128)(2,1)} %collective-permute-done.1), channel_id=1, source_target_pairs={{0,12},{4,0},{8,4},{12,8},{1,13},{5,1},{9,5},{13,9},{2,14},{6,2},{... | collective-permute-start | bytes 3981320 | tf_op jit(solution)/shard_map/ppermute | solution.py:16
  310.0 1.8 copy-start.3
  335.9 17.0 %copy-start.4 = (bf16[256,576]{0,1:T(8,128)(2,1)S(1)}, bf16[256,576]{0,1:T(8,128)(2,1)}, u32[]{:S(2)}) copy-start(bf16[256,576]{0,1:T(8,128)(2,1)} %reduce-scatter.4.cloned.1.call-done) | copy-start | bytes 884740
  336.0 109.0 %all-gather.16.cloned.1.call-start = ((), (), s32[]{:S(2)}) async-start(), calls=%async_computation.11 | async-start | bytes 5529600 | tf_op jit(solution)/shard_map/all_gather | solution.py:130
  336.5 143.5 %all-gather.14.cloned.1.call-start = ((), (), s32[]{:S(2)}) async-start(), calls=%async_computation.10 | async-start | bytes 1843200 | tf_op jit(solution)/shard_map/all_gather | solution.py:124
  337.3 178.7 %all-gather.18.cloned.1.call-start = ((), (), s32[]{:S(2)}) async-start(), calls=%async_computation.12 | async-start | bytes 1843200 | tf_op jit(solution)/shard_map/all_gather | solution.py:137
  354.2 9.5 %copy-start.8 = (s32[4]{0:T(128)S(1)}, s32[4]{0:T(128)}, u32[]{:S(2)}) copy-start(s32[4]{0:T(128)} %param.19) | copy-start | bytes 52
  354.2 9.5 %copy-start.5 = (f32[13,1152]{1,0:T(8,128)S(1)}, f32[13,1152]{1,0:T(8,128)}, u32[]{:S(2)}) copy-start(f32[13,1152]{1,0:T(8,128)} %param.18) | copy-start | bytes 179716
  354.2 9.7 %copy-start.7 = (f32[3,1152]{1,0:T(4,128)S(1)}, f32[3,1152]{1,0:T(4,128)}, u32[]{:S(2)}) copy-start(f32[3,1152]{1,0:T(4,128)} %param.21) | copy-start | bytes 41476
  359.1 92.4 %all-to-all-start = ((bf16[4,2,18432]{2,1,0:T(2,128)(2,1)}), bf16[4,2,18432]{2,1,0:T(2,128)(2,1)S(1)}, u32[]{:S(2)}, u32[]{:S(2)}) async-start(bf16[4,2,18432]{2,1,0:T(2,128)(2,1)} %reshape.175), calls=%async_computation.2 | async-start | bytes 589824 | tf_op jit(solution)/shard_map/all_to_all | solution.py:99
  363.7 166.1 %reduce-scatter.8.cloned.1.call-start = ((), (), s32[]{:S(2)}) async-start(), calls=%async_computation.13 | async-start | bytes 442368 | tf_op jit(solution)/shard_map/reduce_scatter | solution.py:140
Sparse Core Ops, SparseCore 0:
  8.9 87.2 all-gather.7
  97.7 33.7 all-gather.9
  134.6 14.2 reduce-scatter.3
  150.4 146.1 all-gather.11
  336.1 16.8 reduce-scatter.5
  354.4 90.5 all-gather.15
  446.5 33.4 all-gather.13
  481.6 34.2 all-gather.17
  518.8 11.0 reduce-scatter.7
